TPU v7x, 256 devices: a whole 4x4x8 slice. The times are simulated.
256 devices in a mesh: row: 8 (over x, core), col: 32 (over y, z).
Axes of the slice: x: 4, y: 4, z: 8, core: 2. Of those that a mesh axis runs over, the one named last changes fastest.
Arguments:
- affinity_tiles: bfloat16 [1024, 64, 128, 128], P(('row', 'col'))
- block_columns: int32 [1024, 64], P(('row', 'col')), may hold values from 0 to 127, as said below
- live_counts: int32 [8, 128], P('row', 'col'), may hold values from 1 to 64, 4096 in all within a row
- earlier_blocks: float32 [4, 64, 131072], P(None, None, ('row', 'col')), may hold values from -6 to 6
Outputs:
- new_blocks: float32 [2, 64, 131072], P(None, None, ('row', 'col'))
- triangular_factors: float32 [2, 64, 64], replicated
Inputs may be any that keep to these rules, and one draw needn't show every extreme that they name: `block_columns`: slot 0 of every block row names the block row itself; columns name block rows of the same row group. `live_counts`: slots at or past a block row's count are ignored.
All inputs are finite; a program needn't handle non-finite values.
Results may differ from a plain program's by a relative error of at most 0.0059.
Values may be sent and summed in bfloat16 or wider, within the bound.
No kernel may reach another device: no remote copies, remote signals or barrier semaphores. Data moves between devices by JAX's collectives and lax.ppermute only.
A program may use at most 64 MiB of HBM per device.

v0:
```python
import jax
import jax.numpy as jnp
from jax import lax
from jax.sharding import PartitionSpec as P

STEPS = 2


def apply_tiles(affinity_tiles, block_columns, row_counts, group_blocks):
    block_rows = affinity_tiles.shape[0]
    slot_count = affinity_tiles.shape[1]
    tile_size = affinity_tiles.shape[2]
    block_width = group_blocks.shape[0]
    slot_ids = lax.broadcasted_iota(jnp.int32, (block_rows, slot_count), 1)
    live_mask = slot_ids < row_counts[:, None]
    picked = jnp.take(group_blocks, block_columns, axis=1)
    picked = jnp.where(live_mask[None, :, :, None], picked, jnp.zeros((), jnp.bfloat16))
    running = jnp.einsum(
        "rsij,brsj->bri", affinity_tiles, picked, preferred_element_type=jnp.float32
    )
    return running.reshape(block_width, block_rows * tile_size)


def on_device(affinity_tiles, block_columns, live_counts, earlier_blocks):
    block_rows = affinity_tiles.shape[0]
    tile_size = affinity_tiles.shape[2]
    block_width = earlier_blocks.shape[1]
    rows_here = earlier_blocks.shape[2]
    total_rows = rows_here * lax.axis_size("row") * lax.axis_size("col")
    row_counts = live_counts.reshape(block_rows)
    known_list = [earlier_blocks[i] for i in range(earlier_blocks.shape[0])]
    first_half = known_list[-1].astype(jnp.bfloat16)
    group_half = lax.all_gather(first_half, "col", axis=1, tiled=True)
    fresh_list = []
    factor_list = []
    for step_index in range(STEPS):
        is_last = step_index + 1 == STEPS
        group_blocks = group_half.reshape(block_width, -1, tile_size)
        product = apply_tiles(affinity_tiles, block_columns, row_counts, group_blocks)
        known = jnp.concatenate(known_list, 0)
        local_proj = jnp.dot(known, product.T, precision=lax.Precision.HIGHEST) / total_rows
        projections = lax.psum(local_proj, ("row", "col"))
        residual = product - jnp.dot(projections.T, known, precision=lax.Precision.HIGHEST)
        local_gram = jnp.dot(residual, residual.T, precision=lax.Precision.HIGHEST) / total_rows
        gram_sum = lax.psum(local_gram, ("row", "col"))
        factor_low = jnp.linalg.cholesky(gram_sum)
        fresh = jax.scipy.linalg.solve_triangular(factor_low, residual, lower=True)
        fresh_list.append(fresh)
        factor_list.append(factor_low.T)
        known_list.append(fresh)
        if not is_last:
            group_half = lax.all_gather(fresh.astype(jnp.bfloat16), "col", axis=1, tiled=True)
    return (jnp.stack(fresh_list), jnp.stack(factor_list))


def solution(mesh):
    return jax.shard_map(
        on_device,
        mesh=mesh,
        in_specs=(
            P(("row", "col"), None, None, None),
            P(("row", "col"), None),
            P("row", "col"),
            P(None, None, ("row", "col")),
        ),
        out_specs=(P(None, None, ("row", "col")), P()),
        check_vma=False,
    )
```

profile of v0, /device:TPU:1, one launch (start us, length us, event | category | flops | bytes accessed | tf_op | source)
XLA Modules:
  0.0 864.7 jit_solution(17645085274301516106)
XLA Ops:
  7.2 0.0 all-gather.3.cloned.1.call-start
  7.2 1.5 fusion.32
  8.8 0.0 all-gather.3.cloned.1.call-update
  8.8 0.0 all-reduce.3.cloned.1.call-start
  8.8 0.7 compare_select_fusion
  9.5 0.1 reshape.73
  9.6 0.8 iota_compare_fusion.2
  10.4 0.9 constant_dynamic-update-slice_fusion.4
  11.3 0.9 constant_dynamic-update-slice_fusion.3
  12.2 0.9 constant_dynamic-update-slice_fusion.2
  13.1 1.1 slice_bitcast_fusion.2
  14.3 71.6 %all-gather.3.cloned.1.call-done = bf16[64,16384]{1,0:T(8,128)(2,1)} async-done(((bf16[64,512]{1,0:T(8,128)(2,1)}), bf16[64,16384]{1,0:T(8,128)(2,1)}) %all-gather.3.cloned.1.call-update) | async-done | bytes 2097168 | tf_op jit(solution)/shard_map/all_gather | solution.py:33
  85.9 2.2 copy_bitcast_fusion.1
  88.1 3.0 gather_fusion
  91.1 6.3 fusion.12
  97.3 1.2 convolution_multiply_fusion.1
  98.6 0.0 all-reduce.3.cloned.1.call-update
  98.6 0.0 all-gather.5.cloned.1.call-start
  98.6 0.9 constant_dynamic-update-slice_fusion.1
  99.6 246.5 %all-reduce.3.cloned.1.call-done = f32[256,64]{1,0:T(8,128)} async-done(((f32[256,64]{1,0:T(8,128)}), f32[256,64]{1,0:T(8,128)}) %all-reduce.3.cloned.1.call-update) | async-done | bytes 65552 | tf_op jit(solution)/shard_map/psum | solution.py:42
  346.0 1.3 convolution_subtract_fusion.1
  347.3 0.3 convolution_multiply_fusion.3
  347.6 76.2 %psum.29 = f32[64,64]{0,1:T(8,128)S(1)} all-reduce(f32[64,64]{0,1:T(8,128)S(1)} %convolution_multiply_fusion.3), channel_id=1, replica_groups=mesh['row'=8,'col'=32] {'row','col'}, use_global_device_ids=true, to_apply=%region_1.3 | all-reduce | flops 4096 | bytes 32768 | tf_op jit(solution)/shard_map/psum | solution.py:45
  423.8 0.1 copy.16
  423.9 5.8 cholesky.44
  429.8 0.6 compare_reduce_fusion.1
  430.4 0.7 fusion.24
  431.1 4.9 custom-call.6
  436.0 1.0 fusion.33
  437.0 0.0 all-gather.5.cloned.1.call-update
  437.0 0.0 all-reduce.5.cloned.1.call-start
  437.0 66.8 %all-gather.5.cloned.1.call-done = bf16[64,16384]{1,0:T(8,128)(2,1)} async-done(((bf16[64,512]{1,0:T(8,128)(2,1)}), bf16[64,16384]{1,0:T(8,128)(2,1)}) %all-gather.5.cloned.1.call-update) | async-done | bytes 2097168 | tf_op jit(solution)/shard_map/all_gather | solution.py:52
  503.8 2.2 copy_bitcast_fusion
  506.0 3.0 gather_fusion.1
  509.0 6.3 fusion.13
  515.3 1.3 convolution_multiply_fusion
  516.7 251.0 %all-reduce.5.cloned.1.call-done = f32[320,64]{1,0:T(8,128)} async-done(((f32[320,64]{1,0:T(8,128)}), f32[320,64]{1,0:T(8,128)}) %all-reduce.5.cloned.1.call-update) | async-done | bytes 81936 | tf_op jit(solution)/shard_map/psum | solution.py:42
  767.7 1.5 convolution_subtract_fusion
  769.2 0.3 convolution_multiply_fusion.2
  769.4 74.8 %psum.31 = f32[64,64]{0,1:T(8,128)S(1)} all-reduce(f32[64,64]{0,1:T(8,128)S(1)} %convolution_multiply_fusion.2), channel_id=1, replica_groups=mesh['row'=8,'col'=32] {'row','col'}, use_global_device_ids=true, to_apply=%region_5.9 | all-reduce | flops 4096 | bytes 32768 | tf_op jit(solution)/shard_map/psum | solution.py:45
  844.2 0.1 copy.20
  844.3 5.8 cholesky.55
  850.2 0.6 compare_reduce_fusion
  850.8 0.7 fusion.25
  851.5 0.7 copy.21
  852.2 4.9 custom-call.7
  857.1 0.3 convolution_bitcast_fusion
  857.4 0.7 pad_maximum_fusion.3
  (7 shorter events, 0.1 us)
Async XLA Ops:
  7.2 78.7 %all-gather.3.cloned.1.call-start = ((), (), s32[]{:S(2)}) async-start(), calls=%async_computation | async-start | bytes 2162688 | tf_op jit(solution)/shard_map/all_gather | solution.py:33
  8.8 337.2 %all-reduce.3.cloned.1.call-start = ((), (), s32[]{:S(2)}) async-start(), calls=%async_computation.1 | async-start | bytes 262144 | tf_op jit(solution)/shard_map/psum | solution.py:42
  98.6 405.2 %all-gather.5.cloned.1.call-start = ((), (), s32[]{:S(2)}) async-start(), calls=%async_computation.2 | async-start | bytes 2162688 | tf_op jit(solution)/shard_map/all_gather | solution.py:52
  437.0 330.7 %all-reduce.5.cloned.1.call-start = ((), (), s32[]{:S(2)}) async-start(), calls=%async_computation.3 | async-start | bytes 327680 | tf_op jit(solution)/shard_map/psum | solution.py:42
Sparse Core Ops, SparseCore 0:
  11.0 74.8 all-gather.2
  98.7 247.2 all-reduce.2
  437.1 66.6 all-gather.4
  516.8 250.8 all-reduce.4
where the time goes:
time: 865 us
  waiting for transfers between devices  636 us (74%)
  blocking collectives  151 us (17%)
  other arithmetic  26.4 us (3%)
  matrix products  19.7 us (2%)
  local copies, waits for them, and re-layouts  17.7 us (2%)
  between operations  13.9 us (2%)
    psum x2, waiting for transfers between devices, on_device(): projections = lax.psum(local_proj, ('row', 'col'))  497 us
    psum x2, blocking collectives, on_device(): gram_sum = lax.psum(local_gram, ('row', 'col'))  151 us
    all_gather x1, waiting for transfers between devices, on_device(): group_half = lax.all_gather(first_half, 'col', axis=1, tiled=True)  71.6 us
    all_gather x1, waiting for transfers between devices, on_device(): lax.all_gather(fresh.astype(jnp.bfloat16), 'col', axis=1, tiled=True)  66.8 us
  transfers between devices with their start and end apart: 4, of which 4 were waited for; matrix products, arithmetic and copies ran while one was open for 1% of the time, Pallas kernels for 0%

commit v1 on v0

--- a/solution.py
+++ b/solution.py
@@ -1,9 +1,19 @@
+import functools
 import jax
 import jax.numpy as jnp
 from jax import lax
 from jax.sharding import PartitionSpec as P
 
 STEPS = 2
+
+
+def forms_put(packet, ndim_at):
+    base_arr = jnp.stack([packet for _ in range(lax.axis_size("col"))], axis=0)
+    piece_now = jnp.concatenate(lax.all_to_all(base_arr, "col", 0, 0), ndim_at)
+    return piece_now
+
+
+boxes_launch = functools.partial(forms_put, ndim_at=1)
 
 
 def apply_tiles(affinity_tiles, block_columns, row_counts, group_blocks):
@@ -30,7 +40,7 @@
     row_counts = live_counts.reshape(block_rows)
     known_list = [earlier_blocks[i] for i in range(earlier_blocks.shape[0])]
     first_half = known_list[-1].astype(jnp.bfloat16)
-    group_half = lax.all_gather(first_half, "col", axis=1, tiled=True)
+    group_half = boxes_launch(first_half)
     fresh_list = []
     factor_list = []
     for step_index in range(STEPS):

time: 865 us -> 845 us (0.977)
  waiting for transfers between devices: 636 us -> 602 us
  starting transfers between devices: 0.16 us -> 12.3 us
    all_gather x1 -> x0, waiting for transfers between devices: 71.6 us -> none  [on_device(): group_half = lax.all_gather(first_half, 'col', axis=1, tiled=True)]
    all_to_all x0 -> x1, waiting for transfers between devices: none -> 47.9 us  [forms_put(): piece_now = jnp.concatenate(lax.all_to_all(base_arr, 'col', 0, 0), ndim_at)]
    all_to_all x0 -> x1, starting transfers between devices: none -> 12 us  [forms_put(): piece_now = jnp.concatenate(lax.all_to_all(base_arr, 'col', 0, 0), ndim_at)]
    another operation x0 -> x4, local copies, waits for them, and re-layouts: none -> 9.86 us  [the longest x2 7.3 us: on_device(): group_blocks = group_half.reshape(block_width, -1, tile_size)]
    psum x2, waiting for transfers between devices: 497 us -> 488 us  [on_device(): projections = lax.psum(local_proj, ('row', 'col'))]
  transfers between devices with their start and end apart: 4 -> 4, of which waited for: 4 -> 4; matrix products, arithmetic and copies ran while one was open for 1% -> 0% of each run, Pallas kernels for 0% -> 0%
where the time goes in v1:
time: 845 us; the launch traced here: 844 us
  waiting for transfers between devices  602 us (71%)
  blocking collectives  149 us (18%)
  other arithmetic  25 us (3%)
  local copies, waits for them, and re-layouts  22.3 us (3%)
  matrix products  19.7 us (2%)
  between operations  14 us (2%)
  starting transfers between devices  12.3 us (1%)
    psum x2, waiting for transfers between devices, on_device(): projections = lax.psum(local_proj, ('row', 'col'))  488 us
    psum x2, blocking collectives, on_device(): gram_sum = lax.psum(local_gram, ('row', 'col'))  149 us
    all_gather x1, waiting for transfers between devices, on_device(): lax.all_gather(fresh.astype(jnp.bfloat16), 'col', axis=1, tiled=True)  65.5 us
    all_to_all x1, waiting for transfers between devices, forms_put(): piece_now = jnp.concatenate(lax.all_to_all(base_arr, 'col', 0, 0), ndim_at)  47.9 us
  transfers between devices with their start and end apart: 4, of which 4 were waited for; matrix products, arithmetic and copies ran while one was open for 0% of the time, Pallas kernels for 0%

profile of v1, /device:TPU:1, one launch (start us, length us, event | category | flops | bytes accessed | tf_op | source)
XLA Modules:
  0.0 844.0 jit_solution(10965521268150021920)
XLA Ops:
  7.2 1.0 fusion.18
  8.2 1.6 stack.17
  9.8 12.0 %all-to-all-start = ((bf16[32,64,512]{2,1,0:T(8,128)(2,1)}), bf16[32,64,512]{2,1,0:T(8,128)(2,1)S(1)}, u32[]{:S(2)}, u32[]{:S(2)}) async-start(bf16[32,64,512]{2,1,0:T(8,128)(2,1)} %stack.17), calls=%async_computation | async-start | bytes 4194304 | tf_op jit(solution)/shard_map/all_to_all | solution.py:12
  21.8 0.0 all-reduce.3.cloned.1.call-start
  21.9 0.1 reshape.74
  21.9 0.0 copy-done.4
  22.0 0.1 iota_compare_fusion.2
  22.1 0.7 slice_bitcast_fusion.2
  22.8 47.9 %all-to-all-done = bf16[32,64,512]{2,1,0:T(8,128)(2,1)S(1)} async-done(((bf16[32,64,512]{2,1,0:T(8,128)(2,1)}), bf16[32,64,512]{2,1,0:T(8,128)(2,1)S(1)}, u32[]{:S(2)}, u32[]{:S(2)}) %all-to-all-start) | async-done | bytes 2097184 | tf_op jit(solution)/shard_map/all_to_all | solution.py:12
  70.7 2.5 copy.21
  73.2 4.4 reshape_reshape.3
  77.6 2.9 copy.22
  80.5 3.0 gather_fusion
  83.5 6.3 fusion.12
  89.8 0.0 copy-done.1
  89.8 1.2 convolution_multiply_fusion.1
  91.1 0.0 all-reduce.3.cloned.1.call-update
  91.1 0.0 all-gather.2.cloned.1.call-start
  91.2 240.9 %all-reduce.3.cloned.1.call-done = f32[256,64]{0,1:T(8,128)} async-done(((f32[256,64]{0,1:T(8,128)}), f32[256,64]{0,1:T(8,128)}) %all-reduce.3.cloned.1.call-update) | async-done | bytes 65552 | tf_op jit(solution)/shard_map/psum | solution.py:52
  332.1 1.3 convolution_subtract_fusion.1
  333.4 0.3 convolution_multiply_fusion.3
  333.6 74.7 %psum.29 = f32[64,64]{0,1:T(8,128)S(1)} all-reduce(f32[64,64]{0,1:T(8,128)S(1)} %convolution_multiply_fusion.3), channel_id=1, replica_groups=mesh['row'=8,'col'=32] {'row','col'}, use_global_device_ids=true, to_apply=%region_1.3 | all-reduce | flops 4096 | bytes 32768 | tf_op jit(solution)/shard_map/psum | solution.py:55
  408.3 0.1 copy.25
  408.4 5.8 cholesky.44
  414.3 0.6 compare_reduce_fusion.1
  414.9 0.7 fusion.25
  415.6 4.9 custom-call.6
  420.5 1.0 fusion.33
  421.5 0.0 all-gather.2.cloned.1.call-update
  421.5 0.2 all-reduce.5.cloned.1.call-start
  421.7 65.5 %all-gather.2.cloned.1.call-done = bf16[64,16384]{1,0:T(8,128)(2,1)} async-done(((bf16[64,512]{1,0:T(8,128)(2,1)}), bf16[64,16384]{1,0:T(8,128)(2,1)}) %all-gather.2.cloned.1.call-update) | async-done | bytes 2097168 | tf_op jit(solution)/shard_map/all_gather | solution.py:62
  487.2 2.2 copy_bitcast_fusion
  489.3 3.0 gather_fusion.1
  492.4 6.3 fusion.13
  498.6 1.4 convolution_multiply_fusion
  500.0 0.0 all-reduce.5.cloned.1.call-update
  500.0 247.4 %all-reduce.5.cloned.1.call-done = f32[320,64]{0,1:T(8,128)} async-done(((f32[320,64]{0,1:T(8,128)}), f32[320,64]{0,1:T(8,128)}) %all-reduce.5.cloned.1.call-update) | async-done | bytes 81936 | tf_op jit(solution)/shard_map/psum | solution.py:52
  747.4 1.4 convolution_subtract_fusion
  748.9 0.3 convolution_multiply_fusion.2
  749.1 74.4 %psum.31 = f32[64,64]{0,1:T(8,128)S(1)} all-reduce(f32[64,64]{0,1:T(8,128)S(1)} %convolution_multiply_fusion.2), channel_id=1, replica_groups=mesh['row'=8,'col'=32] {'row','col'}, use_global_device_ids=true, to_apply=%region_5.9 | all-reduce | flops 4096 | bytes 32768 | tf_op jit(solution)/shard_map/psum | solution.py:55
  823.5 0.1 copy.29
  823.6 5.8 cholesky.55
  829.5 0.6 compare_reduce_fusion
  830.1 0.7 fusion.26
  830.8 0.7 copy.30
  831.5 4.9 custom-call.7
  836.4 0.3 convolution_bitcast_fusion
  836.8 0.7 pad_maximum_fusion.3
  (19 shorter events, 0.2 us)
Async XLA Ops:
  7.2 14.9 %copy-start = (f32[4,64,512]{2,1,0:T(8,128)S(1)}, f32[4,64,512]{2,1,0:T(8,128)}, u32[]{:S(2)}) copy-start(f32[4,64,512]{2,1,0:T(8,128)} %param.12) | copy-start | bytes 1572868
  7.2 14.7 %copy-start.3 = (s32[4,64]{1,0:T(4,128)S(1)}, s32[4,64]{1,0:T(4,128)}, u32[]{:S(2)}) copy-start(s32[4,64]{1,0:T(4,128)} %param.10) | copy-start | bytes 3076
  7.2 14.8 %copy-start.4 = (s32[1,4]{1,0:T(1,128)S(1)}, s32[1,4]{1,0:T(1,128)}, u32[]{:S(2)}) copy-start(s32[1,4]{1,0:T(1,128)} %param.11) | copy-start | bytes 52
  9.8 60.9 %all-to-all-start = ((bf16[32,64,512]{2,1,0:T(8,128)(2,1)}), bf16[32,64,512]{2,1,0:T(8,128)(2,1)S(1)}, u32[]{:S(2)}, u32[]{:S(2)}) async-start(bf16[32,64,512]{2,1,0:T(8,128)(2,1)} %stack.17), calls=%async_computation | async-start | bytes 4194304 | tf_op jit(solution)/shard_map/all_to_all | solution.py:12
  21.8 310.3 %all-reduce.3.cloned.1.call-start = ((), (), s32[]{:S(2)}) async-start(), calls=%async_computation.1 | async-start | bytes 131072 | tf_op jit(solution)/shard_map/psum | solution.py:52
  83.5 6.3 copy-start.1
  83.5 6.3 copy-start.2
  91.1 396.0 %all-gather.2.cloned.1.call-start = ((), (), s32[]{:S(2)}) async-start(), calls=%async_computation.2 | async-start | bytes 2162688 | tf_op jit(solution)/shard_map/all_gather | solution.py:62
  421.5 325.9 %all-reduce.5.cloned.1.call-start = ((), (), s32[]{:S(2)}) async-start(), calls=%async_computation.3 | async-start | bytes 196608 | tf_op jit(solution)/shard_map/psum | solution.py:52
Sparse Core Ops, SparseCore 0:
  91.2 240.8 all-reduce.2
  421.6 65.5 all-gather.1
  500.1 247.2 all-reduce.4
